TPU v7x, 32 devices: a whole 2x2x4 slice. The times are simulated.
32 devices in a mesh: groups: 2 (over x), chan: 16 (over z, y, core).
Axes of the slice: x: 2, y: 2, z: 4, core: 2. Of those that a mesh axis runs over, the one named last changes fastest.
Arguments:
- samples: bfloat16 [2048, 2, 143, 256], P(('groups', 'chan')), parts along dimension 0, may hold values from -6 to 6
- flags: int32 [2048], P('groups'), parts along dimension 0, may hold values 0 or 1
- delays: int32 [256, 1024], replicated, may hold values from 0 to 255
- order: int32 [2048], P('groups'), parts along dimension 0, may hold values from 0 to 1023, each once
Outputs:
- visibilities: bfloat16 [512, 36, 2, 128, 128], P(('groups', 'chan')), parts along dimension 0
- beam_voltages: bfloat16 [512, 2, 113, 256], P(('groups', 'chan')), parts along dimension 0
There are 2 independent parts, one for each index of `groups`. A program takes and returns all parts, laid end to end along the dimension named above; an argument that names none is the same for every part. Nothing has to cross between parts.
Inputs may be any that keep to these rules, and one draw needn't show every extreme that they name: `order`: each antenna appears once.
All inputs are finite; a program needn't handle non-finite values.
Results may differ from a plain program's by a relative error of at most 0.008.
Values may be sent and summed in bfloat16 or wider, within the bound.
No kernel may reach another device: no remote copies, remote signals or barrier semaphores. Data moves between devices by JAX's collectives and lax.ppermute only.
A program may use at most 128 MiB of HBM per device.

v0:
```python
import math
import jax
import jax.numpy as jnp
import numpy as np
from jax import lax
from jax.sharding import PartitionSpec as P

ANTENNA_INPUTS = 1024
CHANNEL_COUNT = 256
VOLTAGE_BEAMS = 256
TAPS = 16
TILE_ANTENNAS = 128
WINDOW_SPECTRA = 128
OUTFRAMES = 113


def prototype(tap_count, chan_count):
    length = tap_count * chan_count
    counter = jnp.arange(length, dtype=jnp.float32)
    shifted = (counter - (length - 1) / 2.0) / chan_count
    window = 0.5 - 0.5 * jnp.cos(2.0 * math.pi * (counter + 0.5) / length)
    return (jnp.sinc(shifted) * window).reshape(tap_count, chan_count)


def dft_table(chan_count, direction):
    counter = jnp.arange(chan_count, dtype=jnp.int32)
    phase = counter[:, None] * counter[None, :] % chan_count
    angle = phase.astype(jnp.float32) * (2.0 * math.pi / chan_count)
    cosine = jnp.cos(angle)
    sine = jnp.sin(angle)
    top_rows = jnp.stack([cosine, -direction * sine], axis=1)
    bottom_rows = jnp.stack([direction * sine, cosine], axis=1)
    return jnp.stack([top_rows, bottom_rows], axis=0).astype(jnp.bfloat16)


def tile_pairs(tile_count):
    first_tiles = []
    second_tiles = []
    for row_tile in range(tile_count):
        for col_tile in range(row_tile, tile_count):
            first_tiles.append(row_tile)
            second_tiles.append(col_tile)
    return (np.array(first_tiles, np.int32), np.array(second_tiles, np.int32))


def per_device(samples, flags, delays, order):
    device_list = lax.axis_size("chan")
    local_channels = CHANNEL_COUNT // device_list
    local_antennas = samples.shape[0]
    filt = prototype(TAPS, CHANNEL_COUNT)
    filtered_frames = jnp.zeros((local_antennas, 2, WINDOW_SPECTRA, CHANNEL_COUNT), jnp.float32)
    for tap_step in range(TAPS):
        filtered_frames = (
            filtered_frames
            + filt[tap_step] * samples[:, :, tap_step : tap_step + WINDOW_SPECTRA, :]
        )
    filtered_frames = filtered_frames.astype(jnp.bfloat16)
    forward = dft_table(CHANNEL_COUNT, 1.0)
    channel_spectra = jnp.einsum(
        "arsj,rjuk->kaus", filtered_frames, forward, preferred_element_type=jnp.float32
    )
    channel_spectra = (channel_spectra * (1.0 / math.sqrt(CHANNEL_COUNT))).astype(jnp.bfloat16)
    channel_spectra = channel_spectra.reshape(
        device_list, local_channels, local_antennas, 2 * WINDOW_SPECTRA
    )
    flag_values = flags.astype(jnp.bfloat16)
    permuted_flags = jnp.take(flag_values, order, axis=0)
    tile_count = ANTENNA_INPUTS // TILE_ANTENNAS
    first_tiles, second_tiles = tile_pairs(tile_count)

    def correlate_channel(channel_rows):
        other = jnp.concatenate(
            [channel_rows[:, WINDOW_SPECTRA:], -channel_rows[:, :WINDOW_SPECTRA]], axis=1
        )
        stacked = jnp.stack([channel_rows, other], axis=0).reshape(
            2, tile_count, TILE_ANTENNAS, 2 * WINDOW_SPECTRA
        )
        picked = stacked[:, first_tiles]
        columns = channel_rows.reshape(tile_count, TILE_ANTENNAS, 2 * WINDOW_SPECTRA)[second_tiles]
        product = jnp.einsum("upis,pjs->puij", picked, columns, preferred_element_type=jnp.float32)
        return (product * (1.0 / WINDOW_SPECTRA)).astype(jnp.bfloat16)

    received = lax.all_to_all(channel_spectra, "chan", split_axis=0, concat_axis=2, tiled=True)
    turned_rows = received[0]
    permuted = jnp.take(turned_rows, order, axis=1) * permuted_flags[None, :, None]
    visibilities = lax.map(correlate_channel, permuted)
    masked = turned_rows * flag_values[None, :, None]
    other = jnp.concatenate([masked[:, :, WINDOW_SPECTRA:], -masked[:, :, :WINDOW_SPECTRA]], axis=2)
    stacked = jnp.concatenate([masked, other], axis=1)
    channel_ids = lax.axis_index("chan") * local_channels + jnp.arange(
        local_channels, dtype=jnp.int32
    )
    phase = delays[None, :, :] * channel_ids[:, None, None] % CHANNEL_COUNT
    angle = phase.astype(jnp.float32) * (2.0 * math.pi / CHANNEL_COUNT)
    weights = jnp.concatenate([jnp.cos(angle), jnp.sin(angle)], axis=2).astype(jnp.bfloat16)
    formed_beams = jnp.einsum("cba,cas->cbs", weights, stacked, preferred_element_type=jnp.float32)
    beams = (
        (formed_beams * (1.0 / math.sqrt(ANTENNA_INPUTS)))
        .astype(jnp.bfloat16)
        .reshape(local_channels, VOLTAGE_BEAMS, 2, WINDOW_SPECTRA)
    )
    inverse = dft_table(CHANNEL_COUNT, -1.0)
    arranged = lax.all_to_all(beams, "chan", split_axis=1, concat_axis=0, tiled=True)
    result = jnp.einsum("kbrs,rkuj->busj", arranged, inverse, preferred_element_type=jnp.float32)
    zeta = (result * (1.0 / math.sqrt(CHANNEL_COUNT))).astype(jnp.bfloat16)
    beam_local = zeta.shape[0]
    output = jnp.zeros((beam_local, 2, OUTFRAMES, CHANNEL_COUNT), jnp.float32)
    for tap_step in range(TAPS):
        output = output + filt[TAPS - 1 - tap_step] * zeta[:, :, tap_step : tap_step + OUTFRAMES, :]
    return (visibilities, output.astype(jnp.bfloat16))


def solution(mesh):
    in_specs = (P(("groups", "chan"), None, None, None), P("groups"), P(), P("groups"))
    out_specs = (
        P(("groups", "chan"), None, None, None, None),
        P(("groups", "chan"), None, None, None),
    )
    return jax.shard_map(
        per_device, mesh=mesh, in_specs=in_specs, out_specs=out_specs, check_vma=False
    )
```

profile of v0, /device:TPU:0, one launch (start us, length us, event | category | flops | bytes accessed | tf_op | source)
XLA Modules:
  0.0 672.2 jit_solution(12600181944661369911)
XLA Ops:
  3.7 115.9 %add_convert_fusion = bf16[64,2,128,256]{3,1,2,0:T(2,128)(2,1)S(1)} fusion(bf16[64,2,143,256]{3,1,2,0:T(2,128)(2,1)} %param.10, f32[256]{0:T(256)S(1)} %get-tuple-element.109, f32[256]{0:T(256)S(1)} %get-tuple-element.110, f32[256]{0:T(256)S(1)} %get-tuple-element.111, f32[256]{0:T(256)S(1)} %get-tuple-element.112, f32[256]{0:T(256)S(1)} %get-tuple-element.113, ...), kind=kLoop, calls=%fused_computation.37 | loop fusion | flops 201326592 | bytes 142622720 | tf_op jit(solution)/shard_map/convert_element_type | solution.py:57
  119.6 5.3 fusion.22
  124.9 20.5 %copy.30 = bf16[256,64,2,128]{3,2,1,0:T(2,128)(2,1)} copy(bf16[256,64,2,128]{3,0,1,2:T(8,128)(2,1)S(1)} %fusion.22) | data formatting | bytes 16777216 | tf_op jit(solution)/shard_map/convert_element_type | solution.py:62
  145.4 14.1 %reshape.195 = bf16[16,16,64,256]{3,2,1,0:T(8,128)(2,1)} reshape(bf16[256,64,2,128]{3,2,1,0:T(2,128)(2,1)} %copy.30) | data formatting | bytes 16777216 | tf_op jit(solution)/shard_map/reshape | solution.py:63
  159.6 7.6 %all-to-all-start = ((bf16[16,16,64,256]{3,2,1,0:T(8,128)(2,1)}), bf16[16,16,64,256]{3,2,1,0:T(8,128)(2,1)}, u32[]{:S(2)}, u32[]{:S(2)}) async-start(bf16[16,16,64,256]{3,2,1,0:T(8,128)(2,1)} %reshape.195), calls=%async_computation | async-start | bytes 16777216 | tf_op jit(solution)/shard_map/all_to_all | solution.py:83
  167.3 6.8 %gather_fusion.3 = bf16[1024]{0:T(1024)(128)(2,1)S(1)} fusion(bf16[1024]{0:T(1024)(128)(2,1)S(1)} %convert_element_type.187, s32[1024]{0:T(1024)S(1)} %fusion.81), kind=kCustom, calls=%fused_computation.3 | custom fusion | bytes 8192 | tf_op jit(solution)/shard_map/jit(_take)/gather | solution.py:67
  174.1 69.0 %cosine_convert_fusion = (bf16[16,256,1024]{2,1,0:T(8,128)(2,1)}, bf16[16,256,1024]{2,1,0:T(8,128)(2,1)}) fusion(s32[16]{0:T(128)S(1)} %iota_add_fusion.2, s32[256,1024]{1,0:T(8,128)S(1)} %copy-done), kind=kLoop, calls=%fused_computation.36 | loop fusion | flops 67108864 | bytes 17825856 | tf_op jit(solution)/shard_map/convert
  243.1 74.7 %all-to-all-done = bf16[16,16,64,256]{3,2,1,0:T(8,128)(2,1)} async-done(((bf16[16,16,64,256]{3,2,1,0:T(8,128)(2,1)}), bf16[16,16,64,256]{3,2,1,0:T(8,128)(2,1)}, u32[]{:S(2)}, u32[]{:S(2)}) %all-to-all-start) | async-done | bytes 8388640 | tf_op jit(solution)/shard_map/all_to_all | solution.py:83
  317.8 8.3 %copy.31 = bf16[1,16,16,64,256]{4,3,2,1,0:T(8,128)(2,1)} copy(bf16[1,16,16,64,256]{4,3,1,2,0:T(8,128)(2,1)} %bitcast.10) | data formatting | bytes 16777216 | tf_op jit(solution)/shard_map/all_to_all | solution.py:83
  326.0 12.3 %copy.34 = bf16[16,1024,256]{1,2,0:T(8,128)(2,1)} copy(bf16[16,1024,256]{2,1,0:T(8,128)(2,1)} %bitcast.95) | data formatting | bytes 16777216 | tf_op jit(solution)/shard_map/squeeze | solution.py:84
  338.3 11.4 %copy.32 = bf16[16,1024,256]{2,0,1:T(8,128)(2,1)} copy(bf16[16,1024,256]{2,1,0:T(8,128)(2,1)} %bitcast.96) | data formatting | bytes 16777216 | tf_op jit(solution)/shard_map/squeeze | solution.py:84
  349.7 7.1 %broadcast_multiply_fusion = bf16[16,1024,256]{1,2,0:T(8,128)(2,1)} fusion(bf16[16,1024,256]{1,2,0:T(8,128)(2,1)} %copy.34, bf16[1024]{0:T(1024)(128)(2,1)S(1)} %convert_element_type.187), kind=kLoop, calls=%fused_computation.47 | loop fusion | flops 4194304 | bytes 16779264 | tf_op jit(solution)/shard_map/mul | solution.py:87
  361.9 11.3 %multiply_convert_fusion.1 = bf16[16,256,256]{1,2,0:T(8,128)(2,1)S(1)} fusion(bf16[16,1024,128]{1,2,0:T(8,128)(2,1)} %get-tuple-element.99, bf16[16,1024,128]{1,2,0:T(8,128)(2,1)S(1)} %get-tuple-element.98, bf16[16,1024,256]{1,2,0:T(8,128)(2,1)} %broadcast_multiply_fusion, bf16[16,256,1024]{2,1,0:T(8,128)(2,1)} %get-tuple-element.101, ...), kind=kOutput, calls=%fused_computation.46 | convolution fusion | flops 4380950528 | bytes 35651584 | tf_op jit(solution)/shard_map/cba,cas->cbs/dot_general | solution.py:96
  377.3 36.5 %all-to-all-start.1 = ((bf16[16,256,2,128]{3,2,0,1:T(2,128)(2,1)}), bf16[16,256,2,128]{3,2,0,1:T(2,128)(2,1)}, u32[]{:S(2)}, u32[]{:S(2)}) async-start(bf16[16,256,2,128]{3,2,0,1:T(2,128)(2,1)} %copy.35), calls=%async_computation.1 | async-start | bytes 4194304 | tf_op jit(solution)/shard_map/all_to_all | solution.py:103
  413.9 13.1 %gather_fusion.2 = bf16[1024,16,256]{2,1,0:T(8,128)(2,1)} fusion(bf16[16,1024,256]{2,0,1:T(8,128)(2,1)} %copy.32, s32[1024]{0:T(1024)S(1)} %fusion.81), kind=kCustom, calls=%fused_computation.2 | custom fusion | bytes 16781312 | tf_op jit(solution)/shard_map/jit(_take)/gather | solution.py:85
  427.0 10.1 %multiply_bitcast_fusion = bf16[16,1024,256]{2,0,1:T(8,128)(2,1)} fusion(bf16[1024,16,256]{2,1,0:T(8,128)(2,1)} %gather_fusion.2, pred[1024]{0:T(1024)(128)(4,1)S(1)} %get-tuple-element.95, bf16[1024]{0:T(1024)(128)(2,1)S(1)} %get-tuple-element.94), kind=kLoop, calls=%fused_computation.42 | loop fusion | flops 8388608 | bytes 16780288 | tf_op jit(solution)/shard_map/mul | solution.py:85
  437.1 9.7 %copy.33 = bf16[16,1024,256]{2,1,0:T(8,128)(2,1)} copy(bf16[16,1024,256]{2,0,1:T(8,128)(2,1)} %multiply_bitcast_fusion) | data formatting | bytes 16777216
  446.8 205.1 %while.12 = (s32[]{:T(128)}, bf16[16,36,2,128,128]{4,3,2,1,0:T(8,128)(2,1)}, bf16[16,1024,256]{2,1,0:T(8,128)(2,1)}, s32[]{:T(128)}, s32[36]{0:T(128)S(1)}, /*index=5*/s32[36]{0:T(128)S(1)}) while((s32[]{:T(128)}, bf16[16,36,2,128,128]{4,3,2,1,0:T(8,128)(2,1)}, bf16[16,1024,256]{2,1,0:T(8,128)(2,1)}, s32[]{:T(128)}, ...), condition=%wide.region_1.2_spmd.clone.clone, body=%wide.region_0.1_spmd.sunk.clone.clone.sunk | while | flops 608045056 | bytes 29893772 | solution.py:86
  454.4 5.1 fusion.97
  467.3 5.1 fusion.97
  480.1 5.1 fusion.97
  492.9 5.1 fusion.97
  505.7 5.1 fusion.97
  518.5 5.1 fusion.97
  531.4 5.1 fusion.97
  544.2 5.1 fusion.97
  557.0 5.1 fusion.97
  569.8 5.1 fusion.97
  582.6 5.1 fusion.97
  595.4 5.1 fusion.97
  608.3 5.1 fusion.97
  660.5 8.5 %add_convert_fusion.1 = bf16[16,2,113,256]{3,2,0,1:T(8,128)(2,1)S(1)} fusion(bf16[16,2,128,256]{3,2,0,1:T(8,128)(2,1)S(1)} %fusion.34, f32[256]{0:T(256)S(1)} %get-tuple-element.108, f32[256]{0:T(256)S(1)} %get-tuple-element.123, f32[256]{0:T(256)S(1)} %get-tuple-element.122, f32[256]{0:T(256)S(1)} %get-tuple-element.121, f32[256]{0:T(256)S(1)} %get-tuple-element.120, ...), kind=kLoop, calls=%fused_computation.48 | loop fusion | flops 44433408 | bytes 31490048 | tf_op jit(solution)/shard_map/convert_element_type | solution.py:110
  (179 shorter events, 161.6 us)
Async XLA Ops:
  159.6 7.6 %copy-start.6 = (s32[1024]{0:T(1024)S(1)}, s32[1024]{0:T(1024)}, u32[]{:S(2)}) copy-start(s32[1024]{0:T(1024)} %param.11) | copy-start | bytes 12292
  159.6 7.7 %copy-start.3 = (s32[1024]{0:T(1024)S(1)}, s32[1024]{0:T(1024)}, u32[]{:S(2)}) copy-start(s32[1024]{0:T(1024)} %param.13) | copy-start | bytes 12292
  159.6 14.5 %copy-start = (s32[256,1024]{1,0:T(8,128)S(1)}, s32[256,1024]{1,0:T(8,128)}, u32[]{:S(2)}) copy-start(s32[256,1024]{1,0:T(8,128)} %param.12) | copy-start | bytes 3145732
  159.6 158.2 %all-to-all-start = ((bf16[16,16,64,256]{3,2,1,0:T(8,128)(2,1)}), bf16[16,16,64,256]{3,2,1,0:T(8,128)(2,1)}, u32[]{:S(2)}, u32[]{:S(2)}) async-start(bf16[16,16,64,256]{3,2,1,0:T(8,128)(2,1)} %reshape.195), calls=%async_computation | async-start | bytes 16777216 | tf_op jit(solution)/shard_map/all_to_all | solution.py:83
  377.3 274.5 %all-to-all-start.1 = ((bf16[16,256,2,128]{3,2,0,1:T(2,128)(2,1)}), bf16[16,256,2,128]{3,2,0,1:T(2,128)(2,1)}, u32[]{:S(2)}, u32[]{:S(2)}) async-start(bf16[16,256,2,128]{3,2,0,1:T(2,128)(2,1)} %copy.35), calls=%async_computation.1 | async-start | bytes 4194304 | tf_op jit(solution)/shard_map/all_to_all | solution.py:103
  437.1 9.7 %copy-start.4 = (s32[36]{0:T(128)S(1)}, s32[36]{0:T(128)}, u32[]{:S(2)}) copy-start(s32[36]{0:T(128)} %constant.301) | copy-start | bytes 436
  437.1 9.7 %copy-start.5 = (s32[36]{0:T(128)S(1)}, s32[36]{0:T(128)}, u32[]{:S(2)}) copy-start(s32[36]{0:T(128)} %constant.302) | copy-start | bytes 436
  651.8 5.8 copy-start.1
  651.8 5.8 copy-start.2
where the time goes:
time: 675 us; the launch traced here: 672 us
  local copies, waits for them, and re-layouts  227 us (34%)
  other arithmetic  223 us (33%)
  matrix products  102 us (15%)
  waiting for transfers between devices  74.7 us (11%)
  starting transfers between devices  44.2 us (7%)
    convert_element_type x1, other arithmetic, per_device(): filtered_frames = filtered_frames.astype(jnp.bfloat16)  116 us
    dot_general x16, matrix products, correlate_channel(): jnp.einsum('upis,pjs->puij', picked, columns, preferred_element_type=jnp....  82.3 us
    all_to_all x1, waiting for transfers between devices, per_device(): lax.all_to_all(channel_spectra, 'chan', split_axis=0, concat_axis=2, tile...  74.7 us
    gather x16, local copies, waits for them, and re-layouts, correlate_channel(): picked = stacked[:, first_tiles]  72.6 us
    another operation x3, other arithmetic  71.1 us
    all_to_all x1, starting transfers between devices, per_device(): lax.all_to_all(beams, 'chan', split_axis=1, concat_axis=0, tiled=True)  36.5 us
    squeeze x2, local copies, waits for them, and re-layouts, per_device(): turned_rows = received[0]  23.7 us
    convert_element_type x1, local copies, waits for them, and re-layouts, per_device(): (channel_spectra * (1.0 / math.sqrt(CHANNEL_COUNT))).astype(jnp.bfloat16)  20.5 us
  transfers between devices with their start and end apart: 2, of which 1 were waited for; matrix products, arithmetic and copies ran while one was open for 47% of the time, Pallas kernels for 0%

commit v1 on v0

--- a/solution.py
+++ b/solution.py
@@ -4,6 +4,7 @@
 import numpy as np
 from jax import lax
 from jax.sharding import PartitionSpec as P
+from jax.lax import all_to_all, axis_size
 
 ANTENNA_INPUTS = 1024
 CHANNEL_COUNT = 256
@@ -100,7 +101,15 @@
         .reshape(local_channels, VOLTAGE_BEAMS, 2, WINDOW_SPECTRA)
     )
     inverse = dft_table(CHANNEL_COUNT, -1.0)
-    arranged = lax.all_to_all(beams, "chan", split_axis=1, concat_axis=0, tiled=True)
+    arranged = jnp.concatenate(
+        all_to_all(
+            jnp.stack(jnp.split(beams, axis_size("chan"), axis=1)),
+            axis_name="chan",
+            split_axis=0,
+            concat_axis=0,
+        ),
+        axis=0,
+    )
     result = jnp.einsum("kbrs,rkuj->busj", arranged, inverse, preferred_element_type=jnp.float32)
     zeta = (result * (1.0 / math.sqrt(CHANNEL_COUNT))).astype(jnp.bfloat16)
     beam_local = zeta.shape[0]

time: 675 us -> 729 us (1.080)
  local copies, waits for them, and re-layouts: 227 us -> 275 us
    unnamed x16 -> x113, local copies, waits for them, and re-layouts: 12.8 us -> 58.7 us
    split x0 -> x1, local copies, waits for them, and re-layouts: none -> 7.38 us  [per_device(): jnp.split(beams, axis_size('chan'), axis=1)]
  transfers between devices with their start and end apart: 2 -> 2, of which waited for: 1 -> 1; matrix products, arithmetic and copies ran while one was open for 47% -> 44% of each run, Pallas kernels for 0% -> 0%
where the time goes in v1:
time: 729 us; the launch traced here: 719 us
  local copies, waits for them, and re-layouts  275 us (38%)
  other arithmetic  223 us (31%)
  matrix products  100 us (14%)
  waiting for transfers between devices  74.7 us (10%)
  starting transfers between devices  44.8 us (6%)
    convert_element_type x1, other arithmetic, per_device(): filtered_frames = filtered_frames.astype(jnp.bfloat16)  116 us
    dot_general x16, matrix products, correlate_channel(): jnp.einsum('upis,pjs->puij', picked, columns, preferred_element_type=jnp....  82.2 us
    all_to_all x1, waiting for transfers between devices, per_device(): lax.all_to_all(channel_spectra, 'chan', split_axis=0, concat_axis=2, tile...  74.7 us
    gather x16, local copies, waits for them, and re-layouts, correlate_channel(): picked = stacked[:, first_tiles]  73.1 us
    another operation x3, other arithmetic  71.1 us
    unnamed x113, local copies, waits for them, and re-layouts  58.7 us
    all_to_all x1, starting transfers between devices, per_device(): all_to_all(jnp.stack(jnp.split(beams, axis_size('chan'), axis=1)), axis_n...  36.8 us
    squeeze x2, local copies, waits for them, and re-layouts, per_device(): turned_rows = received[0]  23.7 us
  transfers between devices with their start and end apart: 2, of which 1 were waited for; matrix products, arithmetic and copies ran while one was open for 44% of the time, Pallas kernels for 0%

profile of v1, /device:TPU:0, one launch (start us, length us, event | category | flops | bytes accessed | tf_op | source)
XLA Modules:
  0.0 719.4 jit_solution(10455626057562478742)
XLA Ops:
  3.9 115.9 %add_convert_fusion = bf16[64,2,128,256]{3,1,2,0:T(2,128)(2,1)S(1)} fusion(bf16[64,2,143,256]{3,1,2,0:T(2,128)(2,1)} %param.10, f32[256]{0:T(256)S(1)} %get-tuple-element.120, f32[256]{0:T(256)S(1)} %get-tuple-element.121, f32[256]{0:T(256)S(1)} %get-tuple-element.122, f32[256]{0:T(256)S(1)} %get-tuple-element.123, f32[256]{0:T(256)S(1)} %get-tuple-element.124, ...), kind=kLoop, calls=%fused_computation.37 | loop fusion | flops 201326592 | bytes 142622720 | tf_op jit(solution)/shard_map/convert_element_type | solution.py:58
  119.9 5.3 fusion.22
  125.2 20.5 %copy.18 = bf16[256,64,2,128]{3,2,1,0:T(2,128)(2,1)} copy(bf16[256,64,2,128]{3,0,1,2:T(8,128)(2,1)S(1)} %fusion.22) | data formatting | bytes 16777216 | tf_op jit(solution)/shard_map/convert_element_type | solution.py:63
  145.8 14.0 %reshape.198 = bf16[16,16,64,256]{3,2,1,0:T(8,128)(2,1)} reshape(bf16[256,64,2,128]{3,2,1,0:T(2,128)(2,1)} %copy.18) | data formatting | bytes 16777216 | tf_op jit(solution)/shard_map/reshape | solution.py:64
  159.8 8.1 %all-to-all-start = ((bf16[16,16,64,256]{3,2,1,0:T(8,128)(2,1)}), bf16[16,16,64,256]{3,2,1,0:T(8,128)(2,1)}, u32[]{:S(2)}, u32[]{:S(2)}) async-start(bf16[16,16,64,256]{3,2,1,0:T(8,128)(2,1)} %reshape.198), calls=%async_computation | async-start | bytes 16777216 | tf_op jit(solution)/shard_map/all_to_all | solution.py:84
  168.0 6.8 gather_fusion.3
  174.8 69.0 %cosine_convert_fusion = (bf16[16,256,1024]{2,1,0:T(8,128)(2,1)}, bf16[16,256,1024]{2,1,0:T(8,128)(2,1)}) fusion(s32[16]{0:T(128)S(1)} %iota_add_fusion.2, s32[256,1024]{1,0:T(8,128)S(1)} %copy-done), kind=kLoop, calls=%fused_computation.36 | loop fusion | flops 67108864 | bytes 17825856 | tf_op jit(solution)/shard_map/convert
  243.8 74.7 %all-to-all-done = bf16[16,16,64,256]{3,2,1,0:T(8,128)(2,1)} async-done(((bf16[16,16,64,256]{3,2,1,0:T(8,128)(2,1)}), bf16[16,16,64,256]{3,2,1,0:T(8,128)(2,1)}, u32[]{:S(2)}, u32[]{:S(2)}) %all-to-all-start) | async-done | bytes 8388640 | tf_op jit(solution)/shard_map/all_to_all | solution.py:84
  318.4 8.3 %copy.19 = bf16[1,16,16,64,256]{4,3,2,1,0:T(8,128)(2,1)} copy(bf16[1,16,16,64,256]{4,3,1,2,0:T(8,128)(2,1)} %bitcast.10) | data formatting | bytes 16777216 | tf_op jit(solution)/shard_map/all_to_all | solution.py:84
  326.8 12.3 %copy.22 = bf16[16,1024,256]{1,2,0:T(8,128)(2,1)} copy(bf16[16,1024,256]{2,1,0:T(8,128)(2,1)} %bitcast.125) | data formatting | bytes 16777216 | tf_op jit(solution)/shard_map/squeeze | solution.py:85
  339.0 11.4 %copy.20 = bf16[16,1024,256]{2,0,1:T(8,128)(2,1)} copy(bf16[16,1024,256]{2,1,0:T(8,128)(2,1)} %bitcast.126) | data formatting | bytes 16777216 | tf_op jit(solution)/shard_map/squeeze | solution.py:85
  350.5 7.2 broadcast_multiply_fusion
  357.7 5.3 fusion.85
  363.0 11.2 %multiply_convert_fusion.1 = bf16[16,256,256]{1,2,0:T(8,128)(2,1)S(1)} fusion(bf16[16,1024,128]{1,2,0:T(8,128)(2,1)} %get-tuple-element.94, bf16[16,1024,128]{1,2,0:T(8,128)(2,1)S(1)} %get-tuple-element.93, bf16[16,1024,256]{1,2,0:T(8,128)(2,1)} %broadcast_multiply_fusion, bf16[16,256,1024]{2,1,0:T(8,128)(2,1)} %get-tuple-element.112, ...), kind=kOutput, calls=%fused_computation.46 | convolution fusion | flops 4380950528 | bytes 35651584 | tf_op jit(solution)/shard_map/cba,cas->cbs/dot_general | solution.py:97
  374.2 7.4 %fusion.86 = (bf16[16,16,2,128]{1,3,2,0:T(8,128)(2,1)S(1)}, bf16[16,16,2,128]{1,3,2,0:T(8,128)(2,1)S(1)}, bf16[16,16,2,128]{1,3,2,0:T(8,128)(2,1)S(1)}, bf16[16,...) fusion(bf16[16,256,2,128]{1,3,2,0:T(8,128)(2,1)S(1)} %bitcast.124), kind=kLoop, calls=%fused_computation.139 | loop fusion | bytes 4194304 | tf_op jit(solution)/shard_map/split | solution.py:106
  427.9 36.8 %all-to-all-start.1 = ((bf16[16,16,16,2,128]{4,2,3,1,0:T(8,128)(2,1)}), bf16[16,16,16,2,128]{4,2,3,1,0:T(8,128)(2,1)}, u32[]{:S(2)}, u32[]{:S(2)}) async-start(bf16[16,16,16,2,128]{4,2,3,1,0:T(8,128)(2,1)} %bitcast_dynamic-update-slice_fusion), calls=%async_computation.1 | async-start | bytes 4194304 | tf_op jit(solution)/shard_map/all_to_all | solution.py:105
  464.7 12.9 %gather_fusion.2 = bf16[1024,16,256]{2,1,0:T(8,128)(2,1)} fusion(bf16[16,1024,256]{2,0,1:T(8,128)(2,1)} %copy.20, s32[1024]{0:T(1024)S(1)} %fusion.81), kind=kCustom, calls=%fused_computation.2 | custom fusion | bytes 16781312 | tf_op jit(solution)/shard_map/jit(_take)/gather | solution.py:86
  477.6 10.1 %multiply_bitcast_fusion = bf16[16,1024,256]{2,0,1:T(8,128)(2,1)} fusion(bf16[1024,16,256]{2,1,0:T(8,128)(2,1)} %gather_fusion.2, pred[1024]{0:T(1024)(128)(4,1)S(1)} %get-tuple-element.90, bf16[1024]{0:T(1024)(128)(2,1)S(1)} %get-tuple-element.89), kind=kLoop, calls=%fused_computation.42 | loop fusion | flops 8388608 | bytes 16780288 | tf_op jit(solution)/shard_map/mul | solution.py:86
  487.7 9.7 %copy.21 = bf16[16,1024,256]{2,1,0:T(8,128)(2,1)} copy(bf16[16,1024,256]{2,0,1:T(8,128)(2,1)} %multiply_bitcast_fusion) | data formatting | bytes 16777216
  497.5 205.7 %while.12 = (s32[]{:T(128)}, bf16[16,36,2,128,128]{4,3,2,1,0:T(8,128)(2,1)}, bf16[16,1024,256]{2,1,0:T(8,128)(2,1)}, s32[]{:T(128)}, s32[36]{0:T(128)S(1)}, /*index=5*/s32[36]{0:T(128)S(1)}) while((s32[]{:T(128)}, bf16[16,36,2,128,128]{4,3,2,1,0:T(8,128)(2,1)}, bf16[16,1024,256]{2,1,0:T(8,128)(2,1)}, s32[]{:T(128)}, ...), condition=%wide.region_1.2_spmd.clone.clone, body=%wide.region_0.1_spmd.sunk.clone.clone.sunk | while | flops 608045056 | bytes 29893772 | solution.py:87
  505.2 5.1 fusion.98
  518.1 5.1 fusion.98
  531.0 5.1 fusion.98
  543.8 5.1 fusion.98
  556.7 5.1 fusion.98
  569.5 5.1 fusion.98
  582.4 5.1 fusion.98
  595.2 5.1 fusion.98
  608.1 5.1 fusion.98
  620.9 5.1 fusion.98
  633.8 5.1 fusion.98
  707.8 8.2 %add_convert_fusion.1 = bf16[16,2,113,256]{3,2,0,1:T(8,128)(2,1)S(1)} fusion(bf16[16,2,128,256]{3,2,0,1:T(8,128)(2,1)S(1)} %fusion.34, f32[256]{0:T(256)S(1)} %copy-done.8, f32[256]{0:T(256)S(1)} %copy-done.38, f32[256]{0:T(256)S(1)} %copy-done.36, f32[256]{0:T(256)S(1)} %copy-done.34, f32[256]{0:T(256)S(1)} %copy-done.32, f32[256]{0:T(256)S(1)} %copy-done.30, ...), kind=kLoop, calls=%fused_computation.48 | loop fusion | flops 44433408 | bytes 31490048 | tf_op jit(solution)/shard_map/convert_element_type | solution.py:119
  (275 shorter events, 205.4 us)
Async XLA Ops:
  2.8 116.9 %copy-start.7 = (f32[256]{0:T(256)}, f32[256]{0:T(256)S(1)}, u32[]{:S(2)}) copy-start(f32[256]{0:T(256)S(1)} %get-tuple-element.119) | copy-start | bytes 3076
  2.9 116.9 %copy-start.9 = (f32[256]{0:T(256)}, f32[256]{0:T(256)S(1)}, u32[]{:S(2)}) copy-start(f32[256]{0:T(256)S(1)} %get-tuple-element.120) | copy-start | bytes 3076
  2.9 116.9 %copy-start.11 = (f32[256]{0:T(256)}, f32[256]{0:T(256)S(1)}, u32[]{:S(2)}) copy-start(f32[256]{0:T(256)S(1)} %get-tuple-element.121) | copy-start | bytes 3076
  2.9 116.9 %copy-start.13 = (f32[256]{0:T(256)}, f32[256]{0:T(256)S(1)}, u32[]{:S(2)}) copy-start(f32[256]{0:T(256)S(1)} %get-tuple-element.122) | copy-start | bytes 3076
  2.9 116.9 %copy-start.15 = (f32[256]{0:T(256)}, f32[256]{0:T(256)S(1)}, u32[]{:S(2)}) copy-start(f32[256]{0:T(256)S(1)} %get-tuple-element.123) | copy-start | bytes 3076
  2.9 116.9 %copy-start.17 = (f32[256]{0:T(256)}, f32[256]{0:T(256)S(1)}, u32[]{:S(2)}) copy-start(f32[256]{0:T(256)S(1)} %get-tuple-element.124) | copy-start | bytes 3076
  2.9 116.9 %copy-start.19 = (f32[256]{0:T(256)}, f32[256]{0:T(256)S(1)}, u32[]{:S(2)}) copy-start(f32[256]{0:T(256)S(1)} %get-tuple-element.125) | copy-start | bytes 3076
  2.9 116.9 %copy-start.21 = (f32[256]{0:T(256)}, f32[256]{0:T(256)S(1)}, u32[]{:S(2)}) copy-start(f32[256]{0:T(256)S(1)} %get-tuple-element.126) | copy-start | bytes 3076
  2.9 116.9 %copy-start.23 = (f32[256]{0:T(256)}, f32[256]{0:T(256)S(1)}, u32[]{:S(2)}) copy-start(f32[256]{0:T(256)S(1)} %get-tuple-element.127) | copy-start | bytes 3076
  2.9 116.9 %copy-start.25 = (f32[256]{0:T(256)}, f32[256]{0:T(256)S(1)}, u32[]{:S(2)}) copy-start(f32[256]{0:T(256)S(1)} %get-tuple-element.128) | copy-start | bytes 3076
  2.9 116.9 %copy-start.27 = (f32[256]{0:T(256)}, f32[256]{0:T(256)S(1)}, u32[]{:S(2)}) copy-start(f32[256]{0:T(256)S(1)} %get-tuple-element.129) | copy-start | bytes 3076
  3.0 116.9 %copy-start.29 = (f32[256]{0:T(256)}, f32[256]{0:T(256)S(1)}, u32[]{:S(2)}) copy-start(f32[256]{0:T(256)S(1)} %get-tuple-element.130) | copy-start | bytes 3076
  3.0 116.9 %copy-start.31 = (f32[256]{0:T(256)}, f32[256]{0:T(256)S(1)}, u32[]{:S(2)}) copy-start(f32[256]{0:T(256)S(1)} %get-tuple-element.131) | copy-start | bytes 3076
  3.0 116.9 %copy-start.33 = (f32[256]{0:T(256)}, f32[256]{0:T(256)S(1)}, u32[]{:S(2)}) copy-start(f32[256]{0:T(256)S(1)} %get-tuple-element.132) | copy-start | bytes 3076
  3.0 116.9 %copy-start.35 = (f32[256]{0:T(256)}, f32[256]{0:T(256)S(1)}, u32[]{:S(2)}) copy-start(f32[256]{0:T(256)S(1)} %get-tuple-element.133) | copy-start | bytes 3076
  3.0 116.9 %copy-start.37 = (f32[256]{0:T(256)}, f32[256]{0:T(256)S(1)}, u32[]{:S(2)}) copy-start(f32[256]{0:T(256)S(1)} %get-tuple-element.134) | copy-start | bytes 3076
  159.8 8.1 %copy-start.39 = (s32[1024]{0:T(1024)S(1)}, s32[1024]{0:T(1024)}, u32[]{:S(2)}) copy-start(s32[1024]{0:T(1024)} %param.11) | copy-start | bytes 12292
  159.8 8.1 %copy-start.4 = (s32[1024]{0:T(1024)S(1)}, s32[1024]{0:T(1024)}, u32[]{:S(2)}) copy-start(s32[1024]{0:T(1024)} %param.13) | copy-start | bytes 12292
  159.8 15.0 %copy-start = (s32[256,1024]{1,0:T(8,128)S(1)}, s32[256,1024]{1,0:T(8,128)}, u32[]{:S(2)}) copy-start(s32[256,1024]{1,0:T(8,128)} %param.12) | copy-start | bytes 3145732
  159.8 158.6 %all-to-all-start = ((bf16[16,16,64,256]{3,2,1,0:T(8,128)(2,1)}), bf16[16,16,64,256]{3,2,1,0:T(8,128)(2,1)}, u32[]{:S(2)}, u32[]{:S(2)}) async-start(bf16[16,16,64,256]{3,2,1,0:T(8,128)(2,1)} %reshape.198), calls=%async_computation | async-start | bytes 16777216 | tf_op jit(solution)/shard_map/all_to_all | solution.py:84
  409.2 14.8 %copy-start.1 = (bf16[16,16,2,128]{3,1,2,0:T(8,128)(2,1)S(1)}, bf16[16,16,2,128]{3,1,2,0:T(8,128)(2,1)}, u32[]{:S(2)}) copy-start(bf16[16,16,2,128]{3,1,2,0:T(8,128)(2,1)} %copy.59) | copy-start | bytes 393220
  427.9 275.3 %all-to-all-start.1 = ((bf16[16,16,16,2,128]{4,2,3,1,0:T(8,128)(2,1)}), bf16[16,16,16,2,128]{4,2,3,1,0:T(8,128)(2,1)}, u32[]{:S(2)}, u32[]{:S(2)}) async-start(bf16[16,16,16,2,128]{4,2,3,1,0:T(8,128)(2,1)} %bitcast_dynamic-update-slice_fusion), calls=%async_computation.1 | async-start | bytes 4194304 | tf_op jit(solution)/shard_map/all_to_all | solution.py:105
  487.7 9.7 %copy-start.5 = (s32[36]{0:T(128)S(1)}, s32[36]{0:T(128)}, u32[]{:S(2)}) copy-start(s32[36]{0:T(128)} %constant.348) | copy-start | bytes 436
  487.7 9.7 %copy-start.6 = (s32[36]{0:T(128)S(1)}, s32[36]{0:T(128)}, u32[]{:S(2)}) copy-start(s32[36]{0:T(128)} %constant.349) | copy-start | bytes 436
  497.5 208.9 %copy-start.2 = (bf16[1,256,2,256]{1,3,2,0:T(8,128)(2,1)S(1)}, bf16[1,256,2,256]{1,3,2,0:T(8,128)(2,1)}, u32[]{:S(2)}) copy-start(bf16[1,256,2,256]{1,3,2,0:T(8,128)(2,1)} %get-tuple-element.113) | copy-start | bytes 786436
  497.5 208.9 %copy-start.3 = (bf16[1,256,2,256]{1,3,2,0:T(8,128)(2,1)S(1)}, bf16[1,256,2,256]{1,3,2,0:T(8,128)(2,1)}, u32[]{:S(2)}) copy-start(bf16[1,256,2,256]{1,3,2,0:T(8,128)(2,1)} %get-tuple-element.118) | copy-start | bytes 786436
  706.2 1.5 copy-start.8
  706.2 1.5 copy-start.10
  706.2 1.5 copy-start.12
  706.2 1.5 copy-start.14
  706.2 1.5 copy-start.16
  706.2 1.5 copy-start.18
  (10 other events, 14.8 us)
